TPU v7x, 256 devices: a whole 4x4x8 slice. The times are simulated.
256 devices in a mesh: dp: 8 (over x, core), group: 32 (over z, y).
Axes of the slice: x: 4, y: 4, z: 8, core: 2. Of those that a mesh axis runs over, the one named last changes fastest.
Arguments:
- embeds: bfloat16 [65536, 1024], P(('dp', 'group')), may hold values from -6 to 6
- row_ids: int32 [65536], P(('dp', 'group')), may hold values from 0 to 63
- neighbors: int32 [256, 3], P('dp'), may hold values from 0 to 31, as said below
- w_first: bfloat16 [1024, 4096], P(None, 'dp'), may hold values from -0.1875 to 0.1875
- w_second: bfloat16 [4096, 1024], P('dp'), may hold values from -0.09375 to 0.09375
Outputs:
- grad_first: float32 [1024, 4096], P('group', 'dp')
- grad_second: float32 [4096, 1024], P('dp', 'group')
- grad_unit: float32 [65536, 1024], P(('dp', 'group'))
Inputs may be any that keep to these rules, and one draw needn't show every extreme that they name: `neighbors`: within a row the 3 entries differ from one another and from the row's own index b % 32.
All inputs are finite; a program needn't handle non-finite values.
Results may differ from a plain program's by a relative error of at most 0.013.
Values may be sent and summed in bfloat16 or wider, within the bound.
No kernel may reach another device: no remote copies, remote signals or barrier semaphores. Data moves between devices by JAX's collectives and lax.ppermute only.
A program may use at most 64 MiB of HBM per device.

v0:
```python
import jax
import jax.numpy as jnp
from jax import lax
from jax.sharding import PartitionSpec as P

EPS = 1e-06
TEMP = 10.0
SHIFT = -5.0


def gelu_fwd(value):
    return jax.nn.gelu(value, approximate=True)


def gelu_back(pre, grad):
    _, back = jax.vjp(gelu_fwd, pre)
    return back(grad)[0]


def per_device(embeds, row_ids, neighbors, w_first, w_second):
    owners = lax.axis_size("group")
    block = embeds.shape[0]
    piece = block // owners
    width = w_second.shape[1]
    listed = neighbors.shape[1]
    gathered = lax.all_gather(embeds, "dp", axis=0, tiled=True)
    pre = jnp.dot(gathered, w_first, preferred_element_type=jnp.float32)
    hidden = gelu_fwd(pre).astype(jnp.bfloat16)
    proj = lax.psum_scatter(
        jnp.dot(hidden, w_second, preferred_element_type=jnp.float32).astype(jnp.bfloat16),
        "dp",
        scatter_dimension=0,
        tiled=True,
    ).astype(jnp.float32)
    inv = lax.rsqrt(jnp.mean(proj * proj, axis=-1, keepdims=True) + EPS)
    unit = proj * inv
    unit_b = unit.astype(jnp.bfloat16)
    held, held_ids = (
        lax.all_to_all(
            unit_b.reshape(owners, piece, width), "group", split_axis=0, concat_axis=0, tiled=True
        ),
        lax.all_to_all(
            row_ids.reshape(owners, piece), "group", split_axis=0, concat_axis=0, tiled=True
        ),
    )
    order = neighbors.T
    outgoing = jnp.take(held, order, axis=0)
    outgoing_ids = jnp.take(held_ids, order, axis=0)
    fetched, fetched_ids = (
        lax.all_to_all(outgoing, "group", split_axis=1, concat_axis=1, tiled=True),
        lax.all_to_all(outgoing_ids, "group", split_axis=1, concat_axis=1, tiled=True),
    )
    cand = jnp.concatenate([unit_b[None], fetched.reshape(listed, block, width)], 0)
    cand_ids = jnp.concatenate([row_ids[None], fetched_ids.reshape(listed, block)], 0)
    logits = (
        TEMP / width * jnp.einsum("rp,kcp->krc", unit_b, cand, preferred_element_type=jnp.float32)
        + SHIFT
    )
    sign = jnp.where(row_ids[None, :, None] == cand_ids[:, None, :], 1.0, -1.0).astype(jnp.float32)
    weight = (-sign * jax.nn.sigmoid(-sign * logits) * (TEMP / width)).astype(jnp.bfloat16)
    grad_own = jnp.einsum("krc,kcp->rp", weight, cand, preferred_element_type=jnp.float32)
    grad_cand = jnp.einsum("krc,rp->kcp", weight, unit_b, preferred_element_type=jnp.float32)
    returned = lax.all_to_all(
        grad_cand[1:].reshape(listed, owners, piece, width),
        "group",
        split_axis=1,
        concat_axis=1,
        tiled=True,
    )
    select = (order[:, :, None] == jnp.arange(owners, dtype=jnp.int32)[None, None, :]).astype(
        jnp.float32
    )
    summed = jnp.einsum("krb,krqp->bqp", select, returned, precision=lax.Precision.HIGHEST)
    collected = lax.all_to_all(summed, "group", split_axis=0, concat_axis=0, tiled=True)
    grad_unit = grad_own + grad_cand[0] + collected.reshape(block, width)
    grad_proj = inv * (grad_unit - unit * jnp.mean(unit * grad_unit, axis=-1, keepdims=True))
    grad_all = lax.all_gather(grad_proj.astype(jnp.bfloat16), "dp", axis=0, tiled=True)
    second_local = lax.dot_general(
        hidden, grad_all, (((0,), (0,)), ((), ())), preferred_element_type=jnp.float32
    )
    grad_hidden = lax.dot_general(
        grad_all, w_second, (((1,), (1,)), ((), ())), preferred_element_type=jnp.float32
    )
    grad_pre = gelu_back(pre, grad_hidden).astype(jnp.bfloat16)
    first_local = lax.dot_general(
        gathered, grad_pre, (((0,), (0,)), ((), ())), preferred_element_type=jnp.float32
    )
    first_out, second_out = (
        lax.psum_scatter(first_local, "group", scatter_dimension=0, tiled=True),
        lax.psum_scatter(second_local, "group", scatter_dimension=1, tiled=True),
    )
    return (first_out, second_out, grad_unit)


def solution(mesh):
    in_specs = (
        P(("dp", "group"), None),
        P(("dp", "group")),
        P("dp", None),
        P(None, "dp"),
        P("dp", None),
    )
    out_specs = (P("group", "dp"), P("dp", "group"), P(("dp", "group"), None))
    return jax.shard_map(
        per_device, mesh=mesh, in_specs=in_specs, out_specs=out_specs, check_vma=False
    )
```

profile of v0, /device:TPU:4, one launch (start us, length us, event | category | flops | bytes accessed | tf_op | source)
XLA Modules:
  0.0 792.0 jit_solution(12244141082356973376)
XLA Ops:
  8.0 38.2 %all-gather.3.cloned.1.call-done = bf16[2048,1024]{1,0:T(8,128)(2,1)} async-done(((bf16[256,1024]{1,0:T(8,128)(2,1)}), bf16[2048,1024]{1,0:T(8,128)(2,1)}) %all-gather.3.cloned.1.call-update) | async-done | bytes 4194320 | tf_op jit(solution)/shard_map/all_gather | solution.py:26
  46.2 4.8 fusion.58
  51.0 2.0 copy-done.6
  53.0 4.8 convolution_convert_fusion
  58.4 0.7 all_to_all.23
  59.1 9.9 %all-to-all-start = ((s32[32,1,8]{2,1,0:T(1,128)}), s32[32,1,8]{2,1,0:T(1,128)S(1)}, u32[]{:S(2)}, u32[]{:S(2)}) async-start(s32[32,1,8]{2,1,0:T(1,128)} %bitcast.2), calls=%async_computation.1 | async-start | bytes 32768 | tf_op jit(solution)/shard_map/all_to_all | solution.py:42
  69.0 26.2 %reduce-scatter.6.cloned.1.call-done = bf16[256,1024]{1,0:T(8,128)(2,1)} async-done(((bf16[2048,1024]{1,0:T(8,128)(2,1)}), bf16[256,1024]{1,0:T(8,128)(2,1)}) %reduce-scatter.6.cloned.1.call-update) | async-done | bytes 524304 | tf_op jit(solution)/shard_map/reduce_scatter | solution.py:29
  95.2 1.2 fusion.36
  96.4 2.2 fusion.54
  98.6 9.6 %all-to-all-start.2 = ((bf16[32,8,1024]{2,1,0:T(8,128)(2,1)}), bf16[32,8,1024]{2,1,0:T(8,128)(2,1)S(1)}, u32[]{:S(2)}, u32[]{:S(2)}) async-start(bf16[32,8,1024]{2,1,0:T(8,128)(2,1)} %get-tuple-element.19), calls=%async_computation.3 | async-start | bytes 1048576 | tf_op jit(solution)/shard_map/all_to_all | solution.py:39
  109.1 0.7 copy_select_fusion
  109.8 16.9 %all-to-all-done.2 = bf16[32,8,1024]{2,1,0:T(8,128)(2,1)S(1)} async-done(((bf16[32,8,1024]{2,1,0:T(8,128)(2,1)}), bf16[32,8,1024]{2,1,0:T(8,128)(2,1)S(1)}, u32[]{:S(2)}, u32[]{:S(2)}) %all-to-all-start.2) | async-done | bytes 524320 | tf_op jit(solution)/shard_map/all_to_all | solution.py:39
  126.8 4.7 all-to-all-start.1
  131.5 0.7 gather_fusion.1
  132.4 1.3 copy.46
  133.8 7.7 all-to-all-done.1
  141.5 4.0 all-to-all-start.3
  145.6 37.7 %all-to-all-done.3 = bf16[3,32,8,1024]{3,2,0,1:T(8,128)(2,1)S(1)} async-done(((bf16[3,32,8,1024]{3,2,0,1:T(8,128)(2,1)}), bf16[3,32,8,1024]{3,2,0,1:T(8,128)(2,1)S(1)}, u32[]{:S(2)}, u32[]{:S(2)}) %all-to-all-start.3) | async-done | bytes 1572896 | tf_op jit(solution)/shard_map/all_to_all | solution.py:50
  183.5 2.1 fusion.31
  185.6 0.8 fusion.37
  187.2 75.9 %all_to_all.37 = f32[3,32,8,1024]{3,2,0,1:T(8,128)S(1)} all-to-all(f32[3,32,8,1024]{3,2,0,1:T(8,128)S(1)} %copy.50), channel_id=1, replica_groups=mesh['dp'=8,'group'=32] {'group'}, dimensions={1} | all-to-all | bytes 6291456 | tf_op jit(solution)/shard_map/all_to_all | solution.py:63
  263.2 3.1 fusion.14
  266.9 31.0 %all_to_all.38 = f32[32,8,1024]{2,1,0:T(8,128)S(1)} all-to-all(f32[32,8,1024]{2,1,0:T(8,128)S(1)} %copy.52), channel_id=1, replica_groups=mesh['dp'=8,'group'=32] {'group'}, dimensions={0} | all-to-all | bytes 2097152 | tf_op jit(solution)/shard_map/all_to_all | solution.py:74
  297.9 0.9 fusion.32
  298.8 1.0 copy-done.2
  299.8 1.1 fusion.35
  300.9 33.7 %all-gather.5.cloned.1.call-done = bf16[2048,1024]{1,0:T(8,128)(2,1)} async-done(((bf16[256,1024]{1,0:T(8,128)(2,1)}), bf16[2048,1024]{1,0:T(8,128)(2,1)}) %all-gather.5.cloned.1.call-update) | async-done | bytes 4194320 | tf_op jit(solution)/shard_map/all_gather | solution.py:77
  334.6 11.6 %fusion.11 = f32[1024,512]{0,1:T(8,128)S(1)} fusion(bf16[2048,1024]{1,0:T(8,128)(2,1)} %all-gather.3.cloned.1.call-done, f32[2048,512]{1,0:T(8,128)} %copy-done.6, bf16[2048,1024]{1,0:T(8,128)(2,1)} %all-gather.5.cloned.1.call-done, bf16[512,1024]{1,0:T(8,128)(2,1)S(1)} %copy-done), kind=kOutput, calls=%fused_computation.18 | convolution fusion | flops 4315938816 | bytes 15728640 | tf_op jit(solution)/shard_map/dot_general | solution.py:85
  346.2 1.9 copy.56
  348.1 7.3 fusion.55
  355.5 210.5 %reduce-scatter.10.cloned.1.call-done = f32[32,512]{1,0:T(8,128)} async-done(((f32[1024,512]{1,0:T(8,128)}), f32[32,512]{1,0:T(8,128)}) %reduce-scatter.10.cloned.1.call-update) | async-done | bytes 65552
  566.0 219.4 %reduce-scatter.8.cloned.1.call-done = f32[512,32]{0,1:T(8,128)} async-done(((f32[512,1024]{0,1:T(8,128)}), f32[512,32]{0,1:T(8,128)}) %reduce-scatter.8.cloned.1.call-update) | async-done | bytes 65552 | tf_op jit(solution)/shard_map/reduce_scatter | solution.py:90
  (39 shorter events, 4.3 us)
Async XLA Ops:
  7.2 45.8 %copy-start = (bf16[512,1024]{1,0:T(8,128)(2,1)S(1)}, bf16[512,1024]{1,0:T(8,128)(2,1)}, u32[]{:S(2)}) copy-start(bf16[512,1024]{1,0:T(8,128)(2,1)} %param.9) | copy-start | bytes 3145732
  7.2 39.0 %all-gather.3.cloned.1.call-start = ((), (), s32[]{:S(2)}) async-start(), calls=%async_computation.9 | async-start | bytes 4718592 | tf_op jit(solution)/shard_map/all_gather | solution.py:26
  7.9 87.3 %reduce-scatter.6.cloned.1.call-start = ((), (), s32[]{:S(2)}) async-start(), calls=%async_computation.10 | async-start | bytes 4718592 | tf_op jit(solution)/shard_map/reduce_scatter | solution.py:29
  51.0 2.0 copy-start.6
  57.8 0.7 copy-start.5
  57.8 50.5 %copy-start.4 = (s32[32,3]{0,1:T(4,128)S(1)}, s32[32,3]{0,1:T(4,128)}, u32[]{:S(2)}) copy-start(s32[32,3]{0,1:T(4,128)} %param.7) | copy-start | bytes 1156
  59.1 39.5 %all-to-all-start = ((s32[32,1,8]{2,1,0:T(1,128)}), s32[32,1,8]{2,1,0:T(1,128)S(1)}, u32[]{:S(2)}, u32[]{:S(2)}) async-start(s32[32,1,8]{2,1,0:T(1,128)} %bitcast.2), calls=%async_computation.1 | async-start | bytes 32768 | tf_op jit(solution)/shard_map/all_to_all | solution.py:42
  98.6 28.1 %all-to-all-start.2 = ((bf16[32,8,1024]{2,1,0:T(8,128)(2,1)}), bf16[32,8,1024]{2,1,0:T(8,128)(2,1)S(1)}, u32[]{:S(2)}, u32[]{:S(2)}) async-start(bf16[32,8,1024]{2,1,0:T(8,128)(2,1)} %get-tuple-element.19), calls=%async_computation.3 | async-start | bytes 1048576 | tf_op jit(solution)/shard_map/all_to_all | solution.py:39
  126.8 14.7 %all-to-all-start.1 = ((s32[3,32,8]{2,0,1:T(4,128)}), s32[3,32,8]{2,0,1:T(4,128)S(1)}, u32[]{:S(2)}, u32[]{:S(2)}) async-start(s32[3,32,8]{2,0,1:T(4,128)} %copy_select_fusion), calls=%async_computation.2 | async-start | bytes 131072 | tf_op jit(solution)/shard_map/all_to_all | solution.py:51
  132.4 51.0 %copy-start.1 = (bf16[256,1024]{1,0:T(8,128)(2,1)S(1)}, bf16[256,1024]{1,0:T(8,128)(2,1)}, u32[]{:S(2)}) copy-start(bf16[256,1024]{1,0:T(8,128)(2,1)} %reduce-scatter.6.cloned.1.call-done) | copy-start | bytes 1572868
  141.5 41.9 %all-to-all-start.3 = ((bf16[3,32,8,1024]{3,2,0,1:T(8,128)(2,1)}), bf16[3,32,8,1024]{3,2,0,1:T(8,128)(2,1)S(1)}, u32[]{:S(2)}, u32[]{:S(2)}) async-start(bf16[3,32,8,1024]{3,2,0,1:T(8,128)(2,1)} %copy.46), calls=%async_computation.4 | async-start | bytes 3145728 | tf_op jit(solution)/shard_map/all_to_all | solution.py:50
  145.5 189.2 %all-gather.5.cloned.1.call-start = ((), (), s32[]{:S(2)}) async-start(), calls=%async_computation.11 | async-start | bytes 4718592 | tf_op jit(solution)/shard_map/all_gather | solution.py:77
  263.2 34.7 %copy-start.3 = (bf16[1,256,1024]{2,1,0:T(8,128)(2,1)S(1)}, bf16[1,256,1024]{2,1,0:T(8,128)(2,1)}, u32[]{:S(2)}) copy-start(bf16[1,256,1024]{2,1,0:T(8,128)(2,1)} %get-tuple-element.18) | copy-start | bytes 1572868
  298.8 1.0 copy-start.2
  300.9 265.1 %reduce-scatter.10.cloned.1.call-start = ((), (), s32[]{:S(2)}) async-start(), calls=%async_computation.13 | async-start | bytes 2162688
  348.1 437.3 %reduce-scatter.8.cloned.1.call-start = ((), (), s32[]{:S(2)}) async-start(), calls=%async_computation.12 | async-start | bytes 2162688 | tf_op jit(solution)/shard_map/reduce_scatter | solution.py:90
Sparse Core Ops, SparseCore 0:
  9.9 36.2 all-gather.2
  57.9 37.2 reduce-scatter.5
  301.0 33.5 all-gather.4
  348.2 217.7 reduce-scatter.9
  570.7 214.6 reduce-scatter.7
where the time goes:
time: 793 us; the launch traced here: 792 us
  waiting for transfers between devices  591 us (75%)
  blocking collectives  107 us (13%)
  matrix products  35.4 us (4%)
  starting transfers between devices  28.3 us (4%)
  between operations  14 us (2%)
  local copies, waits for them, and re-layouts  10.6 us (1%)
    reduce_scatter x1, waiting for transfers between devices, per_device(): lax.psum_scatter(second_local, 'group', scatter_dimension=1, tiled=True)  219 us
    unnamed x6, waiting for transfers between devices  211 us
    all_to_all x1, blocking collectives, per_device(): lax.all_to_all(grad_cand[1:].reshape(listed, owners, piece, width), 'grou...  75.9 us
    all_gather x1, waiting for transfers between devices, per_device(): gathered = lax.all_gather(embeds, 'dp', axis=0, tiled=True)  38.2 us
    all_to_all x1, waiting for transfers between devices, per_device(): lax.all_to_all(outgoing, 'group', split_axis=1, concat_axis=1, tiled=True)  37.7 us
    all_gather x1, waiting for transfers between devices, per_device(): lax.all_gather(grad_proj.astype(jnp.bfloat16), 'dp', axis=0, tiled=True)  33.7 us
    all_to_all x1, blocking collectives, per_device(): lax.all_to_all(summed, 'group', split_axis=0, concat_axis=0, tiled=True)  31 us
    reduce_scatter x1, waiting for transfers between devices, per_device(): lax.psum_scatter(jnp.dot(hidden, w_second, preferred_element_type=jnp.flo...  26.2 us
  transfers between devices with their start and end apart: 9, of which 8 were waited for; matrix products, arithmetic and copies ran while one was open for 2% of the time, Pallas kernels for 0%

commit v1 on v0

--- a/solution.py
+++ b/solution.py
@@ -47,7 +47,12 @@
     outgoing = jnp.take(held, order, axis=0)
     outgoing_ids = jnp.take(held_ids, order, axis=0)
     fetched, fetched_ids = (
-        lax.all_to_all(outgoing, "group", split_axis=1, concat_axis=1, tiled=True),
+        jnp.concatenate(
+            lax.all_to_all(
+                jnp.stack(jnp.split(outgoing, lax.axis_size("group"), axis=1)), "group", 0, 0
+            ),
+            axis=1,
+        ),
         lax.all_to_all(outgoing_ids, "group", split_axis=1, concat_axis=1, tiled=True),
     )
     cand = jnp.concatenate([unit_b[None], fetched.reshape(listed, block, width)], 0)

time: 793 us -> 792 us (level)
  no operation moved by 1% of the time
where the time goes in v1:
time: 792 us
  waiting for transfers between devices  591 us (75%)
  blocking collectives  107 us (14%)
  matrix products  34.4 us (4%)
  starting transfers between devices  28.6 us (4%)
  between operations  14.2 us (2%)
  local copies, waits for them, and re-layouts  11.6 us (1%)
    reduce_scatter x1, waiting for transfers between devices, per_device(): lax.psum_scatter(second_local, 'group', scatter_dimension=1, tiled=True)  219 us
    unnamed x6, waiting for transfers between devices  211 us
    all_to_all x1, blocking collectives, per_device(): lax.all_to_all(grad_cand[1:].reshape(listed, owners, piece, width), 'grou...  75.9 us
    all_gather x1, waiting for transfers between devices, per_device(): gathered = lax.all_gather(embeds, 'dp', axis=0, tiled=True)  38.2 us
    all_to_all x1, waiting for transfers between devices, per_device(): lax.all_to_all(jnp.stack(jnp.split(outgoing, lax.axis_size('group'), axis...  37.7 us
    all_gather x1, waiting for transfers between devices, per_device(): lax.all_gather(grad_proj.astype(jnp.bfloat16), 'dp', axis=0, tiled=True)  33.8 us
    all_to_all x1, blocking collectives, per_device(): lax.all_to_all(summed, 'group', split_axis=0, concat_axis=0, tiled=True)  31 us
    reduce_scatter x1, waiting for transfers between devices, per_device(): lax.psum_scatter(jnp.dot(hidden, w_second, preferred_element_type=jnp.flo...  26 us
  transfers between devices with their start and end apart: 9, of which 8 were waited for; matrix products, arithmetic and copies ran while one was open for 2% of the time, Pallas kernels for 0%

profile of v1, /device:TPU:4, one launch (start us, length us, event | category | flops | bytes accessed | tf_op | source)
XLA Modules:
  0.0 791.8 jit_solution(4479436548519203982)
XLA Ops:
  8.0 38.2 %all-gather.3.cloned.1.call-done = bf16[2048,1024]{1,0:T(8,128)(2,1)} async-done(((bf16[256,1024]{1,0:T(8,128)(2,1)}), bf16[2048,1024]{1,0:T(8,128)(2,1)}) %all-gather.3.cloned.1.call-update) | async-done | bytes 4194320 | tf_op jit(solution)/shard_map/all_gather | solution.py:26
  46.2 4.8 fusion.58
  51.0 1.9 copy-done.7
  53.0 4.8 convolution_convert_fusion
  59.1 9.8 %all-to-all-start = ((s32[32,1,8]{2,1,0:T(1,128)}), s32[32,1,8]{2,1,0:T(1,128)S(1)}, u32[]{:S(2)}, u32[]{:S(2)}) async-start(s32[32,1,8]{2,1,0:T(1,128)} %bitcast.2), calls=%async_computation.1 | async-start | bytes 32768 | tf_op jit(solution)/shard_map/all_to_all | solution.py:42
  69.0 26.0 %reduce-scatter.6.cloned.1.call-done = bf16[256,1024]{1,0:T(8,128)(2,1)} async-done(((bf16[2048,1024]{1,0:T(8,128)(2,1)}), bf16[256,1024]{1,0:T(8,128)(2,1)}) %reduce-scatter.6.cloned.1.call-update) | async-done | bytes 524304 | tf_op jit(solution)/shard_map/reduce_scatter | solution.py:29
  95.0 1.2 fusion.36
  96.3 2.2 fusion.54
  98.5 9.7 %all-to-all-start.2 = ((bf16[32,8,1024]{2,1,0:T(8,128)(2,1)}), bf16[32,8,1024]{2,1,0:T(8,128)(2,1)S(1)}, u32[]{:S(2)}, u32[]{:S(2)}) async-start(bf16[32,8,1024]{2,1,0:T(8,128)(2,1)} %get-tuple-element.19), calls=%async_computation.3 | async-start | bytes 1048576 | tf_op jit(solution)/shard_map/all_to_all | solution.py:39
  109.0 0.7 copy_select_fusion
  109.8 16.8 %all-to-all-done.2 = bf16[32,8,1024]{2,1,0:T(8,128)(2,1)S(1)} async-done(((bf16[32,8,1024]{2,1,0:T(8,128)(2,1)}), bf16[32,8,1024]{2,1,0:T(8,128)(2,1)S(1)}, u32[]{:S(2)}, u32[]{:S(2)}) %all-to-all-start.2) | async-done | bytes 524320 | tf_op jit(solution)/shard_map/all_to_all | solution.py:39
  126.6 4.9 all-to-all-start.1
  131.5 0.7 gather_fusion.1
  132.9 1.2 copy-done.2
  134.1 7.4 all-to-all-done.1
  141.5 4.0 all-to-all-start.3
  145.6 37.7 %all-to-all-done.3 = bf16[32,3,1,8,1024]{4,3,1,2,0:T(8,128)(2,1)S(1)} async-done(((bf16[32,3,1,8,1024]{4,3,1,2,0:T(8,128)(2,1)}), bf16[32,3,1,8,1024]{4,3,1,2,0:T(8,128)(2,1)S(1)}, u32[]{:S(2)}, u32[]{:S(2)}) %all-to-all-start.3) | async-done | bytes 1572896 | tf_op jit(solution)/shard_map/all_to_all | solution.py:51
  183.5 0.9 copy-done.4
  184.4 1.1 fusion.31
  185.5 0.8 fusion.37
  187.1 75.9 %all_to_all.37 = f32[3,32,8,1024]{3,2,0,1:T(8,128)S(1)} all-to-all(f32[3,32,8,1024]{3,2,0,1:T(8,128)S(1)} %copy.176), channel_id=1, replica_groups=mesh['dp'=8,'group'=32] {'group'}, dimensions={1} | all-to-all | bytes 6291456 | tf_op jit(solution)/shard_map/all_to_all | solution.py:68
  263.0 3.1 fusion.14
  266.7 31.0 %all_to_all.38 = f32[32,8,1024]{2,1,0:T(8,128)S(1)} all-to-all(f32[32,8,1024]{2,1,0:T(8,128)S(1)} %copy.178), channel_id=1, replica_groups=mesh['dp'=8,'group'=32] {'group'}, dimensions={0} | all-to-all | bytes 2097152 | tf_op jit(solution)/shard_map/all_to_all | solution.py:79
  297.7 0.9 fusion.32
  298.7 1.0 copy-done.3
  299.6 1.1 fusion.35
  300.8 33.8 %all-gather.5.cloned.1.call-done = bf16[2048,1024]{1,0:T(8,128)(2,1)} async-done(((bf16[256,1024]{1,0:T(8,128)(2,1)}), bf16[2048,1024]{1,0:T(8,128)(2,1)}) %all-gather.5.cloned.1.call-update) | async-done | bytes 4194320 | tf_op jit(solution)/shard_map/all_gather | solution.py:82
  334.6 11.6 %fusion.11 = f32[1024,512]{0,1:T(8,128)S(1)} fusion(bf16[2048,1024]{1,0:T(8,128)(2,1)} %all-gather.3.cloned.1.call-done, f32[2048,512]{1,0:T(8,128)} %copy-done.7, bf16[2048,1024]{1,0:T(8,128)(2,1)} %all-gather.5.cloned.1.call-done, bf16[512,1024]{1,0:T(8,128)(2,1)S(1)} %copy-done), kind=kOutput, calls=%fused_computation.18 | convolution fusion | flops 4315938816 | bytes 15728640 | tf_op jit(solution)/shard_map/dot_general | solution.py:90
  346.2 1.9 copy.182
  348.2 7.3 fusion.55
  355.5 210.4 %reduce-scatter.10.cloned.1.call-done = f32[32,512]{1,0:T(8,128)} async-done(((f32[1024,512]{1,0:T(8,128)}), f32[32,512]{1,0:T(8,128)}) %reduce-scatter.10.cloned.1.call-update) | async-done | bytes 65552
  565.9 219.3 %reduce-scatter.8.cloned.1.call-done = f32[512,32]{0,1:T(8,128)} async-done(((f32[512,1024]{0,1:T(8,128)}), f32[512,32]{0,1:T(8,128)}) %reduce-scatter.8.cloned.1.call-update) | async-done | bytes 65552 | tf_op jit(solution)/shard_map/reduce_scatter | solution.py:95
  (72 shorter events, 5.2 us)
Async XLA Ops:
  7.2 45.8 %copy-start = (bf16[512,1024]{1,0:T(8,128)(2,1)S(1)}, bf16[512,1024]{1,0:T(8,128)(2,1)}, u32[]{:S(2)}) copy-start(bf16[512,1024]{1,0:T(8,128)(2,1)} %param.9) | copy-start | bytes 3145732
  7.2 39.0 %all-gather.3.cloned.1.call-start = ((), (), s32[]{:S(2)}) async-start(), calls=%async_computation.9 | async-start | bytes 4718592 | tf_op jit(solution)/shard_map/all_gather | solution.py:26
  7.9 87.1 %reduce-scatter.6.cloned.1.call-start = ((), (), s32[]{:S(2)}) async-start(), calls=%async_computation.10 | async-start | bytes 4718592 | tf_op jit(solution)/shard_map/reduce_scatter | solution.py:29
  51.0 2.0 copy-start.7
  57.7 0.7 copy-start.6
  59.1 39.4 %all-to-all-start = ((s32[32,1,8]{2,1,0:T(1,128)}), s32[32,1,8]{2,1,0:T(1,128)S(1)}, u32[]{:S(2)}, u32[]{:S(2)}) async-start(s32[32,1,8]{2,1,0:T(1,128)} %bitcast.2), calls=%async_computation.1 | async-start | bytes 32768 | tf_op jit(solution)/shard_map/all_to_all | solution.py:42
  69.0 39.2 %copy-start.5 = (s32[32,3]{0,1:T(4,128)S(1)}, s32[32,3]{0,1:T(4,128)}, u32[]{:S(2)}) copy-start(s32[32,3]{0,1:T(4,128)} %param.7) | copy-start | bytes 1156
  98.5 28.1 %all-to-all-start.2 = ((bf16[32,8,1024]{2,1,0:T(8,128)(2,1)}), bf16[32,8,1024]{2,1,0:T(8,128)(2,1)S(1)}, u32[]{:S(2)}, u32[]{:S(2)}) async-start(bf16[32,8,1024]{2,1,0:T(8,128)(2,1)} %get-tuple-element.19), calls=%async_computation.3 | async-start | bytes 1048576 | tf_op jit(solution)/shard_map/all_to_all | solution.py:39
  126.6 14.9 %all-to-all-start.1 = ((s32[3,32,8]{2,0,1:T(4,128)}), s32[3,32,8]{2,0,1:T(4,128)S(1)}, u32[]{:S(2)}, u32[]{:S(2)}) async-start(s32[3,32,8]{2,0,1:T(4,128)} %copy_select_fusion), calls=%async_computation.2 | async-start | bytes 131072 | tf_op jit(solution)/shard_map/all_to_all | solution.py:56
  132.9 1.2 copy-start.2
  141.5 41.9 %all-to-all-start.3 = ((bf16[32,3,1,8,1024]{4,3,1,2,0:T(8,128)(2,1)}), bf16[32,3,1,8,1024]{4,3,1,2,0:T(8,128)(2,1)S(1)}, u32[]{:S(2)}, u32[]{:S(2)}) async-start(bf16[32,3,1,8,1024]{4,3,1,2,0:T(8,128)(2,1)} %copy-done.2), calls=%async_computation.4 | async-start | bytes 3145728 | tf_op jit(solution)/shard_map/all_to_all | solution.py:51
  145.4 189.2 %all-gather.5.cloned.1.call-start = ((), (), s32[]{:S(2)}) async-start(), calls=%async_computation.11 | async-start | bytes 4718592 | tf_op jit(solution)/shard_map/all_gather | solution.py:82
  145.6 37.9 %copy-start.1 = (bf16[256,1024]{1,0:T(8,128)(2,1)S(1)}, bf16[256,1024]{1,0:T(8,128)(2,1)}, u32[]{:S(2)}) copy-start(bf16[256,1024]{1,0:T(8,128)(2,1)} %reduce-scatter.6.cloned.1.call-done) | copy-start | bytes 1572868
  183.3 1.0 copy-start.4
  298.6 1.0 copy-start.3
  300.7 265.2 %reduce-scatter.10.cloned.1.call-start = ((), (), s32[]{:S(2)}) async-start(), calls=%async_computation.13 | async-start | bytes 2162688
  348.1 437.1 %reduce-scatter.8.cloned.1.call-start = ((), (), s32[]{:S(2)}) async-start(), calls=%async_computation.12 | async-start | bytes 2162688 | tf_op jit(solution)/shard_map/reduce_scatter | solution.py:95
Sparse Core Ops, SparseCore 0:
  9.9 36.2 all-gather.2
  57.9 37.0 reduce-scatter.5
  300.9 33.7 all-gather.4
  348.2 217.6 reduce-scatter.9
  570.6 214.5 reduce-scatter.7
